TPU v7x, 1024 devices: a whole 4x8x16 slice. The times are simulated.
1024 devices in a mesh: row: 32 (over z, core), col: 8 (over y), rep: 4 (over x).
Axes of the slice: x: 4, y: 8, z: 16, core: 2. Of those that a mesh axis runs over, the one named last changes fastest.
Arguments:
- momentum: float32 [4, 8192, 8192], P('rep', 'row', 'col'), may hold values from -6 to 6
- gradient: bfloat16 [4, 8192, 8192], P('rep', 'row', 'col'), may hold values from -6 to 6
- weight: float32 [8192, 8192], P('row', 'col'), may hold values from -0.0625 to 0.0625
- right_basis: float32 [8192, 256], P('col'), may hold values from -6 to 6
Outputs:
- new_momentum: float32 [4, 8192, 8192], P('rep', 'row', 'col')
- new_weight: float32 [8192, 8192], P('row', 'col')
- new_basis: float32 [8192, 256], P('col')
All inputs are finite; a program needn't handle non-finite values.
Results may differ from a plain program's by a relative error of at most 0.0012.
Values sent between devices are 32-bit elements; how exact they have to be, the bound alone decides.
A program may use at most 32 MiB of HBM per device.

v0:
```python
import jax
import jax.numpy as jnp
from jax import lax
from jax.sharding import PartitionSpec as P

D = 8192
RANK = 256
ITERS = 2


beta_mom = 0.95
learn_rate = 0.05


def on_device(momentum, gradient, weight, right_basis):
    highest = lax.Precision.HIGHEST
    replicas = lax.axis_size("rep")
    buffer = momentum[0] + gradient[0].astype(jnp.float32)
    basis_now = right_basis
    ortho = None
    factor = None
    for sweep in range(ITERS):
        left_part = (
            jnp.dot(buffer, basis_now, precision=highest, preferred_element_type=jnp.float32)
            / replicas
        )
        left = lax.psum(left_part, ("col", "rep"))
        gram_part = jnp.dot(left.T, left, precision=highest, preferred_element_type=jnp.float32)
        gram_full = lax.psum(gram_part, "row")
        low_factor = jnp.linalg.cholesky(gram_full)
        ortho = jax.scipy.linalg.solve_triangular(low_factor, left.T, lower=True).T
        factor_part = (
            jnp.dot(buffer.T, ortho, precision=highest, preferred_element_type=jnp.float32)
            / replicas
        )
        wide_piece = lax.psum_scatter(factor_part, ("row", "rep"), scatter_dimension=0, tiled=True)
        square_sum = lax.psum(jnp.sum(wide_piece * wide_piece, axis=0), ("row", "col", "rep"))
        factor = lax.all_gather(wide_piece, ("row", "rep"), axis=0, tiled=True)
        rms_cols = jnp.sqrt(square_sum / jnp.float32(D) + 1e-06)
        basis_now = factor / rms_cols
    feedback = jnp.dot(ortho, factor.T, precision=highest, preferred_element_type=jnp.float32)
    new_momentum = (buffer - (1.0 - beta_mom) * feedback)[None]
    update = jnp.dot(ortho, basis_now.T, precision=highest, preferred_element_type=jnp.float32)
    new_weight = weight - learn_rate * jnp.sqrt(jnp.float32(D) / jnp.float32(RANK)) * update
    return (new_momentum, new_weight, basis_now)


def solution(mesh):
    return jax.shard_map(
        on_device,
        mesh=mesh,
        in_specs=(P("rep", "row", "col"), P("rep", "row", "col"), P("row", "col"), P("col", None)),
        out_specs=(P("rep", "row", "col"), P("row", "col"), P("col", None)),
        check_vma=False,
    )
```

profile of v0, /device:TPU:1, one launch (start us, length us, event | category | flops | bytes accessed | tf_op | source)
XLA Modules:
  0.0 1765.1 jit_solution(2413739446989840645)
XLA Ops:
  7.2 1.2 copy-done
  8.4 3.1 convolution_multiply_fusion.5
  11.6 0.0 all-reduce.8.cloned.1.call-start
  11.6 181.6 %all-reduce.6.cloned.1.call-done = f32[256,256]{1,0:T(8,128)} async-done(((f32[256,256]{1,0:T(8,128)}), f32[256,256]{1,0:T(8,128)}) %all-reduce.6.cloned.1.call-update) | async-done | bytes 262160 | tf_op jit(solution)/shard_map/psum | solution.py:27
  193.2 2.3 fusion.38
  195.6 0.0 reduce-scatter.3.cloned.1.call-start
  195.6 216.3 %all-reduce.8.cloned.1.call-done = f32[256,256]{0,1:T(8,128)} async-done(((f32[256,256]{0,1:T(8,128)}), f32[256,256]{0,1:T(8,128)}) %all-reduce.8.cloned.1.call-update) | async-done | bytes 262160 | tf_op jit(solution)/shard_map/psum | solution.py:29
  411.9 1.1 copy.8
  413.1 11.7 cholesky.130
  424.9 9.8 custom-call.13
  434.7 0.2 constant_dynamic-update-slice_fusion.3
  434.9 0.3 convolution_subtract_fusion.3
  435.2 11.7 cholesky.147
  447.0 0.7 compare_reduce_fusion.2
  449.0 0.1 triangular_solve.75
  449.1 4.4 while.4
  449.6 0.6 fusion.57
  450.2 1.4 bitcast_dynamic-update-slice_fusion.4
  451.6 0.6 fusion.57
  452.2 1.4 bitcast_dynamic-update-slice_fusion.4
  453.5 19.7 %custom-call.14 = f32[2,128,128]{1,2,0:T(8,128)S(1)} custom-call(f32[2,128,128]{2,1,0:T(8,128)S(1)} %get-tuple-element.19), custom_call_target="InvertDiagBlocksLowerTriangular" | custom-call | tf_op jit(solution)/shard_map/jit(_solve_triangular)/triangular_solve | solution.py:31
  473.2 0.3 fusion.16
  473.5 0.4 convolution_subtract_fusion.1
  473.9 0.3 fusion.23
  474.3 2.8 convolution_multiply_fusion.3
  477.1 0.0 all-gather.3.cloned.1.call-start
  477.1 258.2 %reduce-scatter.3.cloned.1.call-done = f32[8,256]{1,0:T(8,128)} async-done(((f32[1024,256]{1,0:T(8,128)}), f32[8,256]{1,0:T(8,128)}) %reduce-scatter.3.cloned.1.call-update) | async-done | bytes 8208 | tf_op jit(solution)/shard_map/reduce_scatter | solution.py:36
  735.3 0.0 all-reduce.10.cloned.1.call-start
  735.4 0.6 copy-done.10
  736.0 129.8 %psum.44 = f32[256]{0:T(256)S(1)} all-reduce(f32[256]{0:T(256)S(1)} %multiply_reduce_fusion.1), channel_id=1, replica_groups=mesh['row'=32,'col'=8,'rep'=4] {'row','col','rep'}, use_global_device_ids=true, to_apply=%region_8.0 | all-reduce | flops 256 | bytes 2048 | tf_op jit(solution)/shard_map/psum | solution.py:37
  865.9 20.6 %all-gather.3.cloned.1.call-done = f32[1024,256]{1,0:T(8,128)} async-done(((f32[8,256]{1,0:T(8,128)}), f32[1024,256]{1,0:T(8,128)}) %all-gather.3.cloned.1.call-update) | async-done | bytes 1048592 | tf_op jit(solution)/shard_map/all_gather | solution.py:38
  886.5 3.0 convolution_multiply_fusion.4
  889.6 0.0 all-reduce.12.cloned.1.call-start
  889.6 168.3 %all-reduce.10.cloned.1.call-done = f32[256,256]{1,0:T(8,128)} async-done(((f32[256,256]{1,0:T(8,128)}), f32[256,256]{1,0:T(8,128)}) %all-reduce.10.cloned.1.call-update) | async-done | bytes 262160 | tf_op jit(solution)/shard_map/psum | solution.py:27
  1057.9 2.3 fusion.39
  1060.3 0.2 reduce-scatter.5.cloned.1.call-start
  1060.5 216.1 %all-reduce.12.cloned.1.call-done = f32[256,256]{0,1:T(8,128)} async-done(((f32[256,256]{0,1:T(8,128)}), f32[256,256]{0,1:T(8,128)}) %all-reduce.12.cloned.1.call-update) | async-done | bytes 262160 | tf_op jit(solution)/shard_map/psum | solution.py:29
  1276.6 1.1 copy.10
  1277.8 11.7 cholesky.164
  1289.5 0.6 compare_reduce_fusion.1
  1290.2 9.8 custom-call.15
  1300.0 0.2 constant_dynamic-update-slice_fusion.1
  1300.2 0.3 convolution_subtract_fusion.2
  1300.5 11.7 cholesky.181
  1312.2 0.6 compare_reduce_fusion
  1314.3 4.2 while.5
  1314.5 0.6 fusion.58
  1315.1 1.4 bitcast_dynamic-update-slice_fusion.5
  1316.5 0.6 fusion.58
  1317.1 1.4 bitcast_dynamic-update-slice_fusion.5
  1318.5 19.7 %custom-call.16 = f32[2,128,128]{1,2,0:T(8,128)S(1)} custom-call(f32[2,128,128]{2,1,0:T(8,128)S(1)} %get-tuple-element.20), custom_call_target="InvertDiagBlocksLowerTriangular" | custom-call | tf_op jit(solution)/shard_map/jit(_solve_triangular)/triangular_solve | solution.py:31
  1338.2 0.3 fusion.14
  1338.5 0.4 convolution_subtract_fusion
  1338.9 0.3 fusion.19
  1339.2 2.8 convolution_multiply_fusion.2
  1342.0 0.0 all-gather.5.cloned.1.call-start
  1342.1 258.2 %reduce-scatter.5.cloned.1.call-done = f32[8,256]{1,0:T(8,128)} async-done(((f32[1024,256]{1,0:T(8,128)}), f32[8,256]{1,0:T(8,128)}) %reduce-scatter.5.cloned.1.call-update) | async-done | bytes 8208 | tf_op jit(solution)/shard_map/reduce_scatter | solution.py:36
  1600.3 0.7 copy-done.11
  1601.0 129.8 %psum.47 = f32[256]{0:T(256)S(1)} all-reduce(f32[256]{0:T(256)S(1)} %multiply_reduce_fusion), channel_id=1, replica_groups=mesh['row'=32,'col'=8,'rep'=4] {'row','col','rep'}, use_global_device_ids=true, to_apply=%region_13.16 | all-reduce | flops 256 | bytes 2048 | tf_op jit(solution)/shard_map/psum | solution.py:37
  1730.8 20.0 %all-gather.5.cloned.1.call-done = f32[1024,256]{1,0:T(8,128)} async-done(((f32[8,256]{1,0:T(8,128)}), f32[1024,256]{1,0:T(8,128)}) %all-gather.5.cloned.1.call-update) | async-done | bytes 1048592 | tf_op jit(solution)/shard_map/all_gather | solution.py:38
  1750.8 1.4 broadcast_divide_fusion
  1752.2 0.1 copy-done.9
  1752.4 2.8 fusion
  1755.2 2.8 fusion.2
  (52 shorter events, 0.6 us)
Async XLA Ops:
  7.2 1.2 copy-start
  7.2 186.0 %all-reduce.6.cloned.1.call-start = ((), (), s32[]{:S(2)}) async-start(), calls=%async_computation.2 | async-start | bytes 524288 | tf_op jit(solution)/shard_map/psum | solution.py:27
  11.6 400.4 %all-reduce.8.cloned.1.call-start = ((), (), s32[]{:S(2)}) async-start(), calls=%async_computation.3 | async-start | bytes 524288 | tf_op jit(solution)/shard_map/psum | solution.py:29
  195.6 539.7 %reduce-scatter.3.cloned.1.call-start = ((), (), s32[]{:S(2)}) async-start(), calls=%async_computation.4 | async-start | bytes 1056768 | tf_op jit(solution)/shard_map/reduce_scatter | solution.py:36
  411.9 1.2 copy-start.7
  448.9 24.3 %copy-start.5 = (f32[256,256]{1,0:T(8,128)S(1)}, f32[256,256]{1,0:T(8,128)}, u32[]{:S(2)}) copy-start(f32[256,256]{1,0:T(8,128)} %all-reduce.6.cloned.1.call-done) | copy-start | bytes 786436
  449.0 25.3 %copy-start.2 = (bf16[1,256,1024]{2,1,0:T(8,128)(2,1)S(1)}, bf16[1,256,1024]{2,1,0:T(8,128)(2,1)}, u32[]{:S(2)}) copy-start(bf16[1,256,1024]{2,1,0:T(8,128)(2,1)} %param.8) | copy-start | bytes 1572868
  449.0 25.3 %copy-start.1 = (f32[1,256,1024]{2,1,0:T(8,128)S(1)}, f32[1,256,1024]{2,1,0:T(8,128)}, u32[]{:S(2)}) copy-start(f32[1,256,1024]{2,1,0:T(8,128)} %param.7) | copy-start | bytes 3145732
  477.1 409.4 %all-gather.3.cloned.1.call-start = ((), (), s32[]{:S(2)}) async-start(), calls=%async_computation.5 | async-start | bytes 1056768 | tf_op jit(solution)/shard_map/all_gather | solution.py:38
  735.3 0.7 copy-start.10
  735.3 322.6 %all-reduce.10.cloned.1.call-start = ((), (), s32[]{:S(2)}) async-start(), calls=%async_computation.6 | async-start | bytes 524288 | tf_op jit(solution)/shard_map/psum | solution.py:27
  889.6 387.0 %all-reduce.12.cloned.1.call-start = ((), (), s32[]{:S(2)}) async-start(), calls=%async_computation.7 | async-start | bytes 524288 | tf_op jit(solution)/shard_map/psum | solution.py:29
  1060.3 540.0 %reduce-scatter.5.cloned.1.call-start = ((), (), s32[]{:S(2)}) async-start(), calls=%async_computation.8 | async-start | bytes 1056768 | tf_op jit(solution)/shard_map/reduce_scatter | solution.py:36
  1276.6 1.2 copy-start.8
  1314.2 23.9 %copy-start.6 = (f32[256,256]{1,0:T(8,128)S(1)}, f32[256,256]{1,0:T(8,128)}, u32[]{:S(2)}) copy-start(f32[256,256]{1,0:T(8,128)} %all-reduce.10.cloned.1.call-done) | copy-start | bytes 786436
  1342.0 408.8 %all-gather.5.cloned.1.call-start = ((), (), s32[]{:S(2)}) async-start(), calls=%async_computation.9 | async-start | bytes 1056768 | tf_op jit(solution)/shard_map/all_gather | solution.py:38
  1600.3 0.7 copy-start.11
  1750.8 1.5 copy-start.9
  1752.4 2.8 copy-start.3
  1752.4 2.8 copy-start.4
Sparse Core Ops, SparseCore 0:
  12.0 181.1 all-reduce.5
  196.1 215.7 all-reduce.7
  477.2 258.0 reduce-scatter.2
  740.0 146.4 all-gather.2
  890.8 167.0 all-reduce.9
  1060.8 215.7 all-reduce.11
  1342.1 258.0 reduce-scatter.4
  1604.4 146.3 all-gather.4
where the time goes:
time: 1770 us
  waiting for transfers between devices  1340 us (76%)
  blocking collectives  260 us (15%)
  other arithmetic  110 us (6%)
  matrix products  25 us (1%)
    reduce_scatter x2, waiting for transfers between devices, on_device(): lax.psum_scatter(factor_part, ('row', 'rep'), scatter_dimension=0, tiled=...  516 us
    psum x2, waiting for transfers between devices, on_device(): gram_full = lax.psum(gram_part, 'row')  432 us
    psum x2, waiting for transfers between devices, on_device(): left = lax.psum(left_part, ('col', 'rep'))  350 us
    psum x2, blocking collectives, on_device(): lax.psum(jnp.sum(wide_piece * wide_piece, axis=0), ('row', 'col', 'rep'))  260 us
    another operation x13, other arithmetic, on_device(): low_factor = jnp.linalg.cholesky(gram_full)  68.6 us
    all_gather x2, waiting for transfers between devices, on_device(): factor = lax.all_gather(wide_piece, ('row', 'rep'), axis=0, tiled=True)  40.6 us
    another operation x5, other arithmetic, on_device(): ortho = jax.scipy.linalg.solve_triangular(low_factor, left.T, lower=True).T  39.4 us
  transfers between devices with their start and end apart: 8, of which 8 were waited for; matrix products, arithmetic and copies ran while one was open for 0% of the time, Pallas kernels for 0%

commit v1 on v0

v1 whole, which is shorter than its diff:
```python
import functools

import jax
import jax.numpy as jnp
from jax import lax
from jax.experimental import pallas as pl
from jax.experimental.pallas import tpu as pltpu
from jax.sharding import PartitionSpec as P

beta_mom = 0.95
learn_rate = 0.05
CORES = 2
TILE = 8
LANES = 128
HIGHEST = lax.Precision.HIGHEST
MESH = pl.DeviceIdType.MESH


def dot(a, b, over):
    return lax.dot_general(
        a, b, (over, ((), ())), precision=HIGHEST, preferred_element_type=jnp.float32
    )


def rows_by_rows(a, b):
    return dot(a, b, ((1,), (0,)))


def by_transposed(a, b):
    return dot(a, b, ((1,), (1,)))


def transposed_by(a, b):
    return dot(a, b, ((0,), (0,)))


class Cholesky:
    def __init__(self, work):
        self.work = work
        self.n = work.shape[0]
        self.panel = min(128, self.n)

    def load(self, gram):
        n = self.n
        self.work[:, :n] = gram
        eye = lax.broadcasted_iota(jnp.int32, (n, n), 0) == lax.broadcasted_iota(
            jnp.int32, (n, n), 1
        )
        self.work[:, n:] = jnp.where(eye, 1.0, 0.0)

    def blocks(self, first, last):
        work, n, size = self.work, self.n, self.panel
        base = (first * TILE // size) * size
        sub = lax.broadcasted_iota(jnp.int32, (TILE, LANES), 0)
        in_panel = lax.broadcasted_iota(jnp.int32, (size, 1), 0)

        def block(t, carry):
            start = pl.multiple_of(t * TILE, TILE)
            rows = work[pl.ds(start, TILE), :]
            small = pltpu.roll(rows[:, :n], lax.rem(n - start, n), 1)[:, :LANES]
            whole = (TILE, LANES)
            columns = [jnp.broadcast_to(small[:, i : i + 1], whole) for i in range(TILE)]
            a = {
                (r, i): jnp.broadcast_to(columns[i][r : r + 1, :], whole)
                for i in range(TILE)
                for r in range(i, TILE)
            }
            low, inv = {}, {}
            for i in range(TILE):
                root = lax.rsqrt(a[i, i])
                inv[i, i] = root
                for r in range(i + 1, TILE):
                    low[r, i] = a[r, i] * root
                for r in range(i + 1, TILE):
                    for c in range(i + 1, r + 1):
                        a[r, c] = a[r, c] - low[r, i] * low[c, i]
                for c in range(i):
                    acc = low[i, c] * inv[c, c]
                    for k in range(c + 1, i):
                        acc = acc + low[i, k] * inv[k, c]
                    inv[i, c] = -(acc * root)
            sums = [None] * (2 * n // LANES)
            for c in range(TILE):
                column = jnp.where(sub == c, inv[c, c], 0.0)
                for r in range(c + 1, TILE):
                    column = jnp.where(sub == r, inv[r, c], column)
                for k in range(len(sums)):
                    term = column * rows[c : c + 1, k * LANES : (k + 1) * LANES]
                    sums[k] = term if sums[k] is None else sums[k] + term
            rows = jnp.concatenate(sums, axis=1)
            work[pl.ds(start, TILE), :] = rows
            update = transposed_by(rows[:, base : base + size], rows)
            below = in_panel > start + (TILE - 1) - base
            work[base : base + size, :] = work[base : base + size, :] - jnp.where(
                below, update, 0.0
            )
            return carry

        lax.fori_loop(first, last, block, 0)
        end = base + size
        if last * TILE == end and end < n:
            done = work[base:end, :]
            work[end:, :] = work[end:, :] - transposed_by(done[:, end:n], done)

    def inverse(self):
        return self.work[:, self.n :]


def step_kernel(shape, momentum, gradient, basis, ortho_out, factor_out, rms_out, mem, sent, wire):
    reps, cols, depth, m, n, sub, rank, order = shape
    row = lax.axis_index("row")
    core = lax.rem(row, CORES)
    z, y, x = lax.div(row, CORES), lax.axis_index("col"), lax.axis_index("rep")
    half = rank // CORES
    part_x, part_xy, part_z = m // reps, m // reps // cols, sub // depth
    part_g = rank // (reps * cols)
    axes = {
        "x": (reps, x, lambda p: {"rep": p}),
        "y": (cols, y, lambda p: {"col": p}),
        "z": (depth, z, lambda p: {"row": p * CORES + core}),
        "c": (CORES, core, lambda p: {"row": z * CORES + p}),
    }
    used = [0]
    pending = []

    def send(axis, source, target, me_slot):
        size, me, device = axes[axis]
        first = used[0]
        used[0] += size - 1
        for i in range(1, size):
            peer = lax.rem(me + i, size)
            copy = pltpu.make_async_remote_copy(
                src_ref=source(peer),
                dst_ref=target(me_slot),
                send_sem=sent.at[first + i - 1],
                recv_sem=wire.at[first + i - 1],
                device_id=device(peer),
                device_id_type=MESH,
            )
            copy.start()
            pending.append(copy)

        def wait():
            for i in range(1, size):
                origin = lax.rem(me + size - i, size)
                pltpu.make_async_remote_copy(
                    src_ref=source(origin),
                    dst_ref=target(origin),
                    send_sem=sent.at[first + i - 1],
                    recv_sem=wire.at[first + i - 1],
                    device_id=device(origin),
                    device_id_type=MESH,
                ).wait_recv()

        return wait

    barrier = pltpu.get_barrier_semaphore()
    partners = 0
    for size, me, device in axes.values():
        for i in range(1, size):
            pl.semaphore_signal(
                barrier, inc=1, device_id=device(lax.rem(me + i, size)), device_id_type=MESH
            )
            partners += 1

    product = None
    for k in range(reps):
        lanes = slice(k * sub, (k + 1) * sub)
        mem["piece"][k] = momentum[0, :, lanes] + gradient[0, :, lanes].astype(jnp.float32)
        term = rows_by_rows(mem["piece"][k], basis[lanes, :])
        product = term if product is None else product + term
    mem["left_part"][0] = product * (1.0 / reps)
    pl.semaphore_wait(barrier, partners)

    def reduce_left(it):
        part, from_x, from_y = mem["left_part"].at[it], mem["left_x"].at[it], mem["left_y"].at[it]
        all_y, all_x = mem["left_gy"].at[it], mem["left_gx"].at[it]

        def rows_of(p):
            return pl.ds(pl.multiple_of(p * part_x, TILE), part_x)

        wait = send("x", lambda p: part.at[rows_of(p), :], lambda s: from_x.at[s], x)
        from_x[x] = part[rows_of(x), :]
        yield
        wait()
        total = from_x[0]
        for s in range(1, reps):
            total = total + from_x[s]
        mid = mem["left_mid"].at[it]
        mid[...] = total.reshape(cols, part_xy, rank)
        wait = send("y", lambda p: mid.at[p], lambda s: from_y.at[s], y)
        from_y[y] = mid[y]
        yield
        wait()
        total = from_y[0]
        for s in range(1, cols):
            total = total + from_y[s]
        all_y[y] = total
        wait = send("y", lambda p: all_y.at[y], lambda s: all_y.at[s], y)
        yield
        wait()
        all_x[x] = all_y[...]
        wait = send("x", lambda p: all_y, lambda s: all_x.at[s], x)
        yield
        wait()

    def run(stages, fillers=()):
        fillers = list(fillers)
        for number, _ in enumerate(stages):
            if number < len(fillers):
                fillers[number]()

    def left_of(it):
        return mem["left_gx"][it].reshape(m, rank)

    stages = reduce_left(0)
    next(stages)
    exchange = send("x", lambda p: mem["piece"].at[p], lambda s: mem["pieces"].at[s], x)
    mem["pieces"][x] = mem["piece"][x]
    run(stages)
    exchange()
    total = mem["pieces"][0]
    for s in range(1, reps):
        total = total + mem["pieces"][s]
    mem["mean"][...] = total * (1.0 / reps)

    def reduce_right(it, left):
        partial = transposed_by(mem["mean"][...], left)
        mem["gram_part"][it] = transposed_by(left, left)
        mine = pl.multiple_of((x * cols + y) * part_g, TILE)
        gram = mem["gram_part"][it, pl.ds(mine, part_g), :]
        split, other = mem["right_split"].at[it], mem["right_core"].at[it]
        for h in range(CORES):
            lanes = slice(h * half, (h + 1) * half)
            split[h, :sub, :] = partial[:, lanes]
            split[h, sub:, :] = gram[:, lanes]
        wait = send("c", lambda p: split.at[p], lambda s: other.at[0], 0)
        wait()
        both = split[core] + other[0]
        out, got = mem["right_z"].at[it], mem["right_fz"].at[it]
        for s in range(depth):
            out[s, :part_z, :] = both[s * part_z : (s + 1) * part_z, :]
            out[s, part_z:, :] = both[sub:, :]
        wait = send("z", lambda p: out.at[p], lambda s: got.at[s], z)
        got[z] = out[z]
        yield
        wait()
        total = got[0]
        for s in range(1, depth):
            total = total + got[s]
        full, by_y, by_x = mem["right"].at[it], mem["gram_y"].at[it], mem["gram"].at[it]
        full[core, z] = total[:part_z, :]
        wait_z = send("z", lambda p: full.at[core, z], lambda s: full.at[core, s], z)
        by_y[y] = total[part_z:, :]
        wait_y = send("y", lambda p: by_y.at[y], lambda s: by_y.at[s], y)
        yield
        wait_y()
        by_x[core, x] = by_y[...]
        wait_x = send("x", lambda p: by_x.at[core, x], lambda s: by_x.at[core, s], x)
        wait_z()
        wait_c = send("c", lambda p: full.at[core], lambda s: full.at[s], core)
        wait_x()
        wait_g = send("c", lambda p: by_x.at[core], lambda s: by_x.at[s], core)
        yield
        wait_c()
        yield
        wait_g()

    def right_of(it):
        return jnp.concatenate(
            [mem["right"][it, h].reshape(sub, half) for h in range(CORES)], axis=1
        )

    def gram_of(it):
        return jnp.concatenate(
            [mem["gram"][it, h].reshape(rank, half) for h in range(CORES)], axis=1
        )

    def root_mean(it, factor):
        by_x, by_y = mem["square_x"].at[it], mem["square_y"].at[it]
        squares = jnp.sum(factor * factor, axis=0, keepdims=True)
        by_x[x] = jnp.broadcast_to(squares, (TILE, rank))
        wait = send("x", lambda p: by_x.at[x], lambda s: by_x.at[s], x)
        yield
        wait()
        total = by_x[0]
        for s in range(1, reps):
            total = total + by_x[s]
        by_y[y] = total
        wait = send("y", lambda p: by_y.at[y], lambda s: by_y.at[s], y)
        yield
        wait()
        total = by_y[0]
        for s in range(1, cols):
            total = total + by_y[s]
        mem["rms"][it] = jnp.sqrt(total / jnp.float32(order) + 1e-06)

    chol = Cholesky(mem["chol"])
    blocks = rank // TILE

    def some(first, last):
        return functools.partial(chol.blocks, first, last)

    stages = reduce_right(0, left_of(0))
    next(stages)
    next(stages)
    next(stages)
    next(stages)
    right = right_of(0)
    mem["left_part"][1] = rows_by_rows(mem["mean"][...], right)
    for _ in stages:
        pass
    stages_left = reduce_left(1)
    next(stages_left)
    chol.load(gram_of(0))
    quarter = blocks // 4
    some(0, quarter)()
    next(stages_left)
    some(quarter, 2 * quarter)()
    next(stages_left)
    some(2 * quarter, 3 * quarter)()
    next(stages_left)
    some(3 * quarter, blocks)()
    inverse = chol.inverse()
    squares = root_mean(0, by_transposed(right, inverse))
    next(squares)
    for _ in stages_left:
        pass
    left = by_transposed(left_of(1), inverse)
    next(squares)

    stages = reduce_right(1, left)
    next(stages)
    for _ in squares:
        pass
    scale = 1.0 / mem["rms"][0]
    next(stages)
    next(stages)
    next(stages)
    right = right_of(1) * scale[:1, :]
    for _ in stages:
        pass
    mem["scale"][...] = scale
    across = jnp.transpose(jnp.broadcast_to(scale[:1, :], (LANES, rank)))[:, :1]
    chol.load(gram_of(1) * scale[:1, :] * across)
    for i in range(4):
        some(i * quarter, (i + 1) * quarter)()
    inverse = chol.inverse()
    factor = by_transposed(right, inverse)
    mem["factor"][x] = factor
    wait = send("x", lambda p: mem["factor"].at[x], lambda s: mem["factor"].at[s], x)
    squares = root_mean(1, factor)
    next(squares)
    ortho_out[...] = by_transposed(left * mem["scale"][:1, :], inverse)
    next(squares)
    for _ in squares:
        pass
    rms_out[...] = mem["rms"][1]
    wait()
    for k in range(reps):
        factor_out[k * sub : (k + 1) * sub, :] = mem["factor"][k]
    for copy in pending:
        copy.wait_send()
    assert used[0] == sent.shape[0]


def step(mesh, momentum, gradient, weight, right_basis):
    reps, cols = mesh.shape["rep"], mesh.shape["col"]
    depth = mesh.shape["row"] // CORES
    _, m, n = momentum.shape
    sub, rank = n // reps, right_basis.shape[1]
    order = n * cols
    half = rank // CORES
    part_x, part_xy, part_z = m // reps, m // reps // cols, sub // depth
    part_g = rank // (reps * cols)
    f32 = jnp.float32
    shapes = {
        "piece": (reps, m, sub),
        "pieces": (reps, m, sub),
        "mean": (m, sub),
        "left_part": (2, m, rank),
        "left_x": (2, reps, part_x, rank),
        "left_mid": (2, cols, part_xy, rank),
        "left_y": (2, cols, part_xy, rank),
        "left_gy": (2, cols, part_xy, rank),
        "left_gx": (2, reps, cols, part_xy, rank),
        "gram_part": (2, rank, rank),
        "right_split": (2, CORES, sub + part_g, half),
        "right_core": (2, 1, sub + part_g, half),
        "right_z": (2, depth, part_z + part_g, half),
        "right_fz": (2, depth, part_z + part_g, half),
        "right": (2, CORES, depth, part_z, half),
        "gram_y": (2, cols, part_g, half),
        "gram": (2, CORES, reps, cols, part_g, half),
        "square_x": (2, reps, TILE, rank),
        "square_y": (2, cols, TILE, rank),
        "rms": (2, TILE, rank),
        "scale": (TILE, rank),
        "chol": (rank, 2 * rank),
        "factor": (reps, sub, rank),
    }
    links = {"x": reps - 1, "y": cols - 1, "z": depth - 1, "c": CORES - 1}
    left_links = 2 * links["x"] + 2 * links["y"]
    right_links = 2 * links["z"] + links["y"] + links["x"] + 3 * links["c"]
    copies = 2 * (left_links + right_links + links["x"] + links["y"]) + 2 * links["x"]
    vmem = pl.BlockSpec(memory_space=pltpu.VMEM)
    ortho, factor, rms = pl.pallas_call(
        functools.partial(step_kernel, (reps, cols, depth, m, n, sub, rank, order)),
        out_shape=[
            jax.ShapeDtypeStruct((m, rank), f32),
            jax.ShapeDtypeStruct((n, rank), f32),
            jax.ShapeDtypeStruct((TILE, rank), f32),
        ],
        in_specs=[vmem] * 3,
        out_specs=[vmem] * 3,
        scratch_shapes=[
            {name: pltpu.VMEM(dims, f32) for name, dims in shapes.items()},
            pltpu.SemaphoreType.DMA((copies,)),
            pltpu.SemaphoreType.DMA((copies,)),
        ],
        compiler_params=pltpu.CompilerParams(
            collective_id=0, has_side_effects=True, vmem_limit_bytes=40 << 20
        ),
        name="dion_step",
    )(momentum, gradient, right_basis)
    highest = lax.Precision.HIGHEST
    buffer = momentum[0] + gradient[0].astype(f32)
    new_basis = factor / rms[:1, :]
    feedback = jnp.dot(ortho, factor.T, precision=highest, preferred_element_type=f32)
    new_momentum = (buffer - (1.0 - beta_mom) * feedback)[None]
    update = jnp.dot(ortho, new_basis.T, precision=highest, preferred_element_type=f32)
    new_weight = weight - learn_rate * jnp.sqrt(f32(order) / f32(rank)) * update
    return new_momentum, new_weight, new_basis


def solution(mesh):
    return jax.shard_map(
        functools.partial(step, mesh),
        mesh=mesh,
        in_specs=(P("rep", "row", "col"), P("rep", "row", "col"), P("row", "col"), P("col", None)),
        out_specs=(P("rep", "row", "col"), P("row", "col"), P("col", None)),
        check_vma=False,
    )
```

time: 1770 us -> 181 us (0.10)
  waiting for transfers between devices: 1340 us -> 0 us
  blocking collectives: 260 us -> 0 us
  Pallas kernels: 0 us -> 172 us
  other arithmetic: 110 us -> 0.08 us
  matrix products: 25 us -> 4.16 us
    psum x4 -> x0, waiting for transfers between devices: 782 us -> none  [the longest x2 432 us: on_device(): gram_full = lax.psum(gram_part, 'row')]
    reduce_scatter x2 -> x0, waiting for transfers between devices: 516 us -> none  [on_device(): lax.psum_scatter(factor_part, ('row', 'rep'), scatter_dimension=0, tiled=...]
    psum x2 -> x0, blocking collectives: 260 us -> none  [on_device(): lax.psum(jnp.sum(wide_piece * wide_piece, axis=0), ('row', 'col', 'rep'))]
    pallas_call x0 -> x1, Pallas kernels: none -> 172 us  [step(): pl.pallas_call(functools.partial(step_kernel, (reps, cols, depth, m, n, s...]
    another operation x18 -> x0, other arithmetic: 108 us -> none  [the longest x13 68.6 us: on_device(): low_factor = jnp.linalg.cholesky(gram_full)]
    all_gather x2 -> x0, waiting for transfers between devices: 40.6 us -> none  [on_device(): factor = lax.all_gather(wide_piece, ('row', 'rep'), axis=0, tiled=True)]
    dot_general x8 -> x2, matrix products: 22.1 us -> 4.16 us  [the longest x1 2.12 us: step(): jnp.dot(ortho, factor.T, precision=highest, preferred_element_type=f32)]
  transfers between devices with their start and end apart: 8 -> 0, of which waited for: 8 -> 0; matrix products, arithmetic and copies ran while one was open for 0% -> 0% of each run, Pallas kernels for 0% -> 0%
where the time goes in v1:
time: 181 us; the launch traced here: 180 us
  Pallas kernels  172 us (95%)
  matrix products  4.16 us (2%)
  local copies, waits for them, and re-layouts  3.5 us (2%)
    pallas_call x1, Pallas kernels, step(): pl.pallas_call(functools.partial(step_kernel, (reps, cols, depth, m, n, s...  172 us

profile of v1, /device:TPU:1, one launch (start us, length us, event | category | flops | bytes accessed | tf_op | source)
XLA Modules:
  0.0 180.2 jit_solution(13142559266243466086)
XLA Ops:
  0.6 0.0 copy-start
  0.6 1.2 copy-done
  1.9 0.0 copy-start.1
  1.9 1.0 copy-done.1
  2.9 0.0 copy-start.2
  2.9 1.2 copy-done.2
  4.1 171.7 %dion_step.1 = (f32[256,256]{1,0:T(8,128)S(1)}, f32[1024,256]{1,0:T(8,128)S(1)}, f32[8,256]{1,0:T(8,128)S(1)}) custom-call(f32[1,256,1024]{2,1,0:T(8,128)S(1)} %copy-done, bf16[1,256,1024]{2,1,0:T(8,128)(2,1)S(1)} %copy-done.1, f32[1024,256]{1,0:T(8,128)S(1)} %copy-done.2), custom_call_target="tpu_custom_call" | custom-call | tf_op jit(solution)/shard_map/dion_step/pallas_call | solution.py:407
  175.9 0.1 broadcast_divide_fusion
  176.0 0.0 copy-start.3
  176.0 0.0 copy-start.4
  176.0 2.1 %fusion.2 = f32[1,256,1024]{2,1,0:T(8,128)} fusion(f32[256,256]{1,0:T(8,128)S(1)} %get-tuple-element.6, f32[1024,256]{1,0:T(8,128)S(1)} %get-tuple-element.7, f32[1,256,1024]{2,1,0:T(8,128)S(1)} %copy-done, bf16[1,256,1024]{2,1,0:T(8,128)(2,1)S(1)} %copy-done.1), kind=kOutput, calls=%fused_computation.4 | convolution fusion | flops 806354944 | bytes 3932160 | tf_op jit(solution)/shard_map/dot_general | solution.py:429
  178.1 0.0 copy-done.3
  178.1 0.0 copy-done.4
  178.1 2.0 %fusion = f32[256,1024]{1,0:T(8,128)} fusion(f32[256,1024]{1,0:T(8,128)S(1)} %copy-done.4, f32[256,256]{1,0:T(8,128)S(1)} %get-tuple-element.6, f32[1024,256]{1,0:T(8,128)S(1)} %broadcast_divide_fusion), kind=kOutput, calls=%fused_computation.1 | convolution fusion | flops 805830656 | bytes 3407872 | tf_op jit(solution)/shard_map/dot_general | solution.py:431
  (1 shorter events, 0.0 us)
Async XLA Ops:
  0.6 1.2 copy-start
  1.9 1.0 copy-start.1
  2.9 1.2 copy-start.2
  176.0 2.1 %copy-start.3 = (f32[1024,256]{1,0:T(8,128)}, f32[1024,256]{1,0:T(8,128)S(1)}, u32[]{:S(2)}) copy-start(f32[1024,256]{1,0:T(8,128)S(1)} %broadcast_divide_fusion) | copy-start | bytes 3145732
  176.0 2.1 %copy-start.4 = (f32[256,1024]{1,0:T(8,128)S(1)}, f32[256,1024]{1,0:T(8,128)}, u32[]{:S(2)}) copy-start(f32[256,1024]{1,0:T(8,128)} %param.6) | copy-start | bytes 3145732

commit v2 on v0

v2 whole, which is shorter than its diff:
```python
import functools

import jax
import jax.numpy as jnp
from jax import lax
from jax.experimental import pallas as pl
from jax.experimental.pallas import tpu as pltpu
from jax.sharding import PartitionSpec as P

beta_mom = 0.95
learn_rate = 0.05
CORES = 2
TILE = 8
LANES = 128
HIGHEST = lax.Precision.HIGHEST
MESH = pl.DeviceIdType.MESH


def dot(a, b, over):
    return lax.dot_general(
        a, b, (over, ((), ())), precision=HIGHEST, preferred_element_type=jnp.float32
    )


def rows_by_rows(a, b):
    return dot(a, b, ((1,), (0,)))


def by_transposed(a, b):
    return dot(a, b, ((1,), (1,)))


def transposed_by(a, b):
    return dot(a, b, ((0,), (0,)))


def in_three(x):
    high = x.astype(jnp.bfloat16).astype(jnp.float32)
    rest = x - high
    middle = rest.astype(jnp.bfloat16).astype(jnp.float32)
    return high, middle, rest - middle


def thin_product(a, b):
    (ah, am, al), (bh, bm, bl) = in_three(a), in_three(b)
    left = jnp.concatenate([ah, ah, am, am, ah, al], axis=0).astype(jnp.bfloat16)
    right = jnp.concatenate([bh, bm, bh, bm, bl, bh], axis=0).astype(jnp.bfloat16)
    return lax.dot_general(
        left, right, (((0,), (0,)), ((), ())), preferred_element_type=jnp.float32
    )


class Cholesky:
    group = 4

    def __init__(self, work):
        self.work = work
        self.n = work.shape[0]
        self.panel = min(128, self.n)
        self.groups = self.n // (TILE * self.group)

    def load(self, gram):
        n = self.n
        self.work[:, :n] = gram
        eye = lax.broadcasted_iota(jnp.int32, (n, n), 0) == lax.broadcasted_iota(
            jnp.int32, (n, n), 1
        )
        self.work[:, n:] = jnp.where(eye, 1.0, 0.0)

    def run(self, first, last):
        work, n, size, count = self.work, self.n, self.panel, self.group
        step = TILE * count
        base = (first * step // size) * size
        wide = (TILE, LANES)
        tiles = 2 * n // LANES
        sub = lax.broadcasted_iota(jnp.int32, wide, 0)
        in_panel = lax.broadcasted_iota(jnp.int32, (size, 1), 0)

        def spread(block, lane):
            return jnp.broadcast_to(block[:, lane : lane + 1], wide)

        def body(t, carry):
            start = pl.multiple_of(t * step, step)
            rows, small = [], []
            for b in range(count):
                got = work[pl.ds(start + TILE * b, TILE), :]
                rows.append([got[:, k * LANES : (k + 1) * LANES] for k in range(tiles)])
                small.append(pltpu.roll(got[:, :n], lax.rem(n - start, n), 1)[:, :LANES])
            for b in range(count):
                columns = [spread(small[b], TILE * b + i) for i in range(TILE)]
                below = {
                    c: [spread(small[c], TILE * b + i) for i in range(TILE)]
                    for c in range(b + 1, count)
                }
                a = {
                    (r, i): jnp.broadcast_to(columns[i][r : r + 1, :], wide)
                    for i in range(TILE)
                    for r in range(i, TILE)
                }
                low, inv = {}, {}
                for i in range(TILE):
                    root = lax.rsqrt(a[i, i])
                    inv[i, i] = root
                    for r in range(i + 1, TILE):
                        low[r, i] = a[r, i] * root
                    for r in range(i + 1, TILE):
                        for c in range(i + 1, r + 1):
                            a[r, c] = a[r, c] - low[r, i] * low[c, i]
                    for c in range(i):
                        acc = low[i, c] * inv[c, c]
                        for k in range(c + 1, i):
                            acc = acc + low[i, k] * inv[k, c]
                        inv[i, c] = -(acc * root)
                sums = [None] * (tiles + 1)
                source = rows[b] + [small[b]]
                for c in range(TILE):
                    column = jnp.where(sub == c, inv[c, c], 0.0)
                    for r in range(c + 1, TILE):
                        column = jnp.where(sub == r, inv[r, c], column)
                    for k in range(tiles + 1):
                        term = column * source[k][c : c + 1, :]
                        sums[k] = term if sums[k] is None else sums[k] + term
                rows[b], small[b] = sums[:tiles], sums[tiles]
                for c in range(b + 1, count):
                    for i in range(TILE):
                        lower = below[c][0] * inv[i, 0]
                        for k in range(1, i + 1):
                            lower = lower + below[c][k] * inv[i, k]
                        rows[c] = [rows[c][k] - lower * rows[b][k][i : i + 1, :] for k in range(tiles)]
                        small[c] = small[c] - lower * small[b][i : i + 1, :]
            done = jnp.concatenate([jnp.concatenate(r, axis=1) for r in rows], axis=0)
            work[pl.ds(start, step), :] = done
            update = thin_product(done[:, base : base + size], done)
            keep = in_panel > start + (step - 1) - base
            work[base : base + size, :] = work[base : base + size, :] - jnp.where(keep, update, 0.0)
            return carry

        lax.fori_loop(first, last, body, 0)
        end = base + size
        if last * step == end and end < n:
            done = work[base:end, :]
            work[end:, :] = work[end:, :] - transposed_by(done[:, end:n], done)

    def inverse(self):
        return self.work[:, self.n :]


def step_kernel(shape, momentum_in, gradient_in, basis_in, ortho_out, factor_out, rms_out, mem, gradient, local, sent, wire):
    reps, cols, depth, m, n, sub, rank, order = shape
    row = lax.axis_index("row")
    core = lax.rem(row, CORES)
    z, y, x = lax.div(row, CORES), lax.axis_index("col"), lax.axis_index("rep")
    plane = reps * cols
    here = x * cols + y
    half = rank // CORES
    part, part_z, part_g = m // plane, sub // depth, rank // plane

    def far_first(size):
        return sorted(range(1, size), key=lambda i: -min(i, size - i))

    def line(size, me, device):
        return [
            (lax.rem(me + i, size), lax.rem(me + size - i, size), device(lax.rem(me + i, size)))
            for i in far_first(size)
        ]

    def sheet():
        pairs = [(i, j) for i in range(reps) for j in range(cols) if i or j]
        pairs.sort(key=lambda p: -(min(p[0], reps - p[0]) + min(p[1], cols - p[1])))
        out = []
        for i, j in pairs:
            px, py = lax.rem(x + i, reps), lax.rem(y + j, cols)
            ox, oy = lax.rem(x + reps - i, reps), lax.rem(y + cols - j, cols)
            out.append((px * cols + py, ox * cols + oy, {"rep": px, "col": py}))
        return out

    groups = {
        "x": line(reps, x, lambda p: {"rep": p}),
        "y": line(cols, y, lambda p: {"col": p}),
        "z": line(depth, z, lambda p: {"row": p * CORES + core}),
        "c": line(CORES, core, lambda p: {"row": z * CORES + p}),
        "xy": sheet(),
    }
    used = [0]
    pending = []

    def send(group, source, target, mine):
        first = used[0]
        members = groups[group]
        used[0] += len(members)
        for i, (peer, origin, device) in enumerate(members):
            copy = pltpu.make_async_remote_copy(
                src_ref=source(peer),
                dst_ref=target(mine),
                send_sem=sent.at[first + i],
                recv_sem=wire.at[first + i],
                device_id=device,
                device_id_type=MESH,
            )
            copy.start()
            pending.append(copy)

        def wait():
            for i, (peer, origin, device) in enumerate(members):
                pltpu.make_async_remote_copy(
                    src_ref=source(origin),
                    dst_ref=target(origin),
                    send_sem=sent.at[first + i],
                    recv_sem=wire.at[first + i],
                    device_id=device,
                    device_id_type=MESH,
                ).wait_recv()

        return wait

    loads = [
        pltpu.make_async_copy(momentum_in.at[0], mem["momentum"], local.at[0]),
        pltpu.make_async_copy(gradient_in.at[0], gradient, local.at[1]),
        pltpu.make_async_copy(basis_in, mem["basis"], local.at[2]),
    ]
    for load in loads:
        load.start()
    barrier = pltpu.get_barrier_semaphore()
    partners = 0
    for group in ("z", "xy", "c"):
        for _, _, device in groups[group]:
            pl.semaphore_signal(barrier, inc=1, device_id=device, device_id_type=MESH)
            partners += 1
    for load in loads:
        load.wait()

    product = None
    for k in range(reps):
        lanes = slice(k * sub, (k + 1) * sub)
        mem["piece"][k] = mem["momentum"][:, lanes] + gradient[:, lanes].astype(jnp.float32)
        term = rows_by_rows(mem["piece"][k], mem["basis"][lanes, :])
        product = term if product is None else product + term

    def added(ref):
        total = ref[0]
        for s in range(1, ref.shape[0]):
            total = total + ref[s]
        return total

    def scatter_left(it, partial):
        out, got = mem["left_part"].at[it], mem["left_got"].at[it]
        out[...] = partial.reshape(plane, part, rank)
        wait = send("xy", lambda p: out.at[p], lambda s: got.at[s], here)
        got[here] = out[here]
        return wait

    def gather_left(it):
        full = mem["left"].at[it]
        full[here] = added(mem["left_got"].at[it])
        return send("xy", lambda p: full.at[here], lambda s: full.at[s], here)

    def left_of(it):
        return mem["left"][it].reshape(m, rank)

    def reduce_right(it):
        now = mem["now"]
        split, other = mem["right_split"].at[it], mem["right_core"].at[it]
        sibling = CORES - 1 - core

        def lanes_of(h):
            return pl.ds(pl.multiple_of(h * half, half), half)

        mean_t = mem["mean_t"][...]
        split[0] = rows_by_rows(mean_t, now[:, lanes_of(sibling)])
        wait_c = send("c", lambda p: split.at[0], lambda s: other.at[0], 0)
        split[1] = rows_by_rows(mean_t, now[:, lanes_of(core)])
        mem["gram_part"][it] = transposed_by(now[...], now[...])
        mine = pl.ds(pl.multiple_of(here * part_g, TILE), part_g)
        g_out, g_other = mem["gram_split"].at[it], mem["gram_core"].at[it]
        g_out[...] = mem["gram_part"][it, mine, lanes_of(sibling)]
        wait_g = send("c", lambda p: g_out, lambda s: g_other, 0)
        wait_c()
        out, got = mem["right_z"].at[it], mem["right_got"].at[it]
        out[...] = (split[1] + other[0]).reshape(depth, part_z, half)
        wait_c = send("z", lambda p: out.at[p], lambda s: got.at[s], z)
        got[z] = out[z]
        wait_g()
        g_all = mem["gram_z"].at[it]
        g_all[z] = mem["gram_part"][it, mine, lanes_of(core)] + g_other[...]
        wait_g = send("z", lambda p: g_all.at[z], lambda s: g_all.at[s], z)
        yield
        wait_c()
        full = mem["right"].at[it]
        full[core, z] = added(got)
        wait_c = send("z", lambda p: full.at[core, z], lambda s: full.at[core, s], z)
        wait_g()
        gram = mem["gram"].at[it]
        gram[core, here] = added(g_all)
        wait_g = send("xy", lambda p: gram.at[core, here], lambda s: gram.at[core, s], here)
        yield
        wait_c()
        wait_c = send("c", lambda p: full.at[core], lambda s: full.at[s], core)
        wait_g()
        wait_g = send("c", lambda p: gram.at[core], lambda s: gram.at[s], core)
        wait_c()
        yield
        wait_g()

    def joined(ref, rows):
        return jnp.concatenate([ref[h].reshape(rows, half) for h in range(CORES)], axis=1)

    def squares_of(factor):
        squares = jnp.sum(factor * factor, axis=0, keepdims=True)
        return jnp.broadcast_to(squares, (TILE, rank))

    def share(group, name, mine, value):
        ref = mem[name]
        ref[mine] = value
        return send(group, lambda p: ref.at[mine], lambda s: ref.at[s], mine)

    def rms_of(total):
        return jnp.sqrt(total / jnp.float32(order) + 1e-06)

    chol = Cholesky(mem["chol"])
    middle = chol.groups // 2

    pl.semaphore_wait(barrier, partners)
    wait_left = scatter_left(0, product * (1.0 / reps))
    exchange = send("x", lambda p: mem["piece"].at[p], lambda s: mem["pieces"].at[s], x)
    mem["pieces"][x] = mem["piece"][x]
    wait_left()
    wait_left = gather_left(0)
    exchange()
    mem["mean"][...] = added(mem["pieces"]) * (1.0 / reps)
    mem["mean_t"][...] = jnp.transpose(mem["mean"][...])
    wait_left()

    mem["now"][...] = left_of(0)
    stages = reduce_right(0)
    next(stages)
    next(stages)
    next(stages)
    right = joined(mem["right"].at[0], sub)
    wait_left = scatter_left(1, rows_by_rows(mem["mean"][...], right))
    for _ in stages:
        pass
    chol.load(joined(mem["gram"].at[0], rank))
    chol.run(0, middle)
    wait_left()
    wait_left = gather_left(1)
    chol.run(middle, chol.groups)
    inverse = chol.inverse()
    wait_left()
    left = by_transposed(left_of(1), inverse)
    mem["now"][...] = left

    stages = reduce_right(1)
    next(stages)
    squares = squares_of(by_transposed(joined(mem["right"].at[0], sub), inverse))
    wait_squares = share("x", "square_x", x, squares)
    next(stages)
    wait_squares()
    wait_squares = share("y", "square_y", y, added(mem["square_x"]))
    next(stages)
    gathered = mem["rights"]
    gathered[x] = mem["right"][1]
    wait_right = send("x", lambda p: mem["right"].at[1], lambda s: gathered.at[s], x)
    wait_squares()
    scale = (1.0 / rms_of(added(mem["square_y"])))[:1, :]
    mem["scale"][...] = jnp.broadcast_to(scale, (TILE, rank))
    across = jnp.transpose(jnp.broadcast_to(scale, (LANES, rank)))[:, :1]
    for _ in stages:
        pass
    chol.load(joined(mem["gram"].at[1], rank) * scale * across)
    chol.run(0, middle)
    chol.run(middle, chol.groups)
    inverse = chol.inverse()
    scale = mem["scale"][:1, :]
    wait_right()
    squares = None
    for k in range(reps):
        factor = by_transposed(joined(gathered.at[k], sub) * scale, inverse)
        factor_out[k * sub : (k + 1) * sub, :] = factor
        term = squares_of(factor)
        squares = term if squares is None else squares + term
    wait_squares = share("y", "square_last", y, squares)
    ortho_out[...] = by_transposed(mem["now"][...] * scale, inverse)
    for copy in pending:
        copy.wait_send()
    wait_squares()
    rms_out[...] = rms_of(added(mem["square_last"]))
    assert used[0] == sent.shape[0]


def step(mesh, momentum, gradient, weight, right_basis):
    reps, cols = mesh.shape["rep"], mesh.shape["col"]
    depth = mesh.shape["row"] // CORES
    _, m, n = momentum.shape
    sub, rank = n // reps, right_basis.shape[1]
    order = n * cols
    half, plane = rank // CORES, reps * cols
    part, part_z, part_g = m // plane, sub // depth, rank // plane
    f32 = jnp.float32
    shapes = {
        "momentum": (m, n),
        "basis": (n, rank),
        "piece": (reps, m, sub),
        "pieces": (reps, m, sub),
        "mean": (m, sub),
        "mean_t": (sub, m),
        "left_part": (2, plane, part, rank),
        "left_got": (2, plane, part, rank),
        "left": (2, plane, part, rank),
        "now": (m, rank),
        "gram_part": (2, rank, rank),
        "right_split": (2, CORES, sub, half),
        "right_core": (2, 1, sub, half),
        "gram_split": (2, part_g, half),
        "gram_core": (2, part_g, half),
        "right_z": (2, depth, part_z, half),
        "right_got": (2, depth, part_z, half),
        "right": (2, CORES, depth, part_z, half),
        "gram_z": (2, depth, part_g, half),
        "gram": (2, CORES, plane, part_g, half),
        "square_x": (reps, TILE, rank),
        "square_y": (cols, TILE, rank),
        "square_last": (cols, TILE, rank),
        "scale": (TILE, rank),
        "chol": (rank, 2 * rank),
        "rights": (reps, CORES, depth, part_z, half),
    }
    links = {"x": reps - 1, "y": cols - 1, "z": depth - 1, "c": CORES - 1, "xy": plane - 1}
    copies = 2 * (3 * links["xy"] + 3 * links["z"] + 4 * links["c"] + links["x"] + links["y"])
    copies += links["x"]
    hbm = pl.BlockSpec(memory_space=pl.ANY)
    vmem = pl.BlockSpec(memory_space=pltpu.VMEM)
    ortho, factor, rms = pl.pallas_call(
        functools.partial(step_kernel, (reps, cols, depth, m, n, sub, rank, order)),
        out_shape=[
            jax.ShapeDtypeStruct((m, rank), f32),
            jax.ShapeDtypeStruct((n, rank), f32),
            jax.ShapeDtypeStruct((TILE, rank), f32),
        ],
        in_specs=[hbm] * 3,
        out_specs=[vmem] * 3,
        scratch_shapes=[
            {name: pltpu.VMEM(dims, f32) for name, dims in shapes.items()},
            pltpu.VMEM((m, n), gradient.dtype),
            pltpu.SemaphoreType.DMA((3,)),
            pltpu.SemaphoreType.DMA((copies,)),
            pltpu.SemaphoreType.DMA((copies,)),
        ],
        compiler_params=pltpu.CompilerParams(
            collective_id=0, has_side_effects=True, vmem_limit_bytes=58 << 20
        ),
        name="dion_step",
    )(momentum, gradient, right_basis)
    highest = lax.Precision.HIGHEST
    buffer = momentum[0] + gradient[0].astype(f32)
    new_basis = factor / rms[:1, :]
    feedback = jnp.dot(ortho, factor.T, precision=highest, preferred_element_type=f32)
    new_momentum = (buffer - (1.0 - beta_mom) * feedback)[None]
    update = jnp.dot(ortho, new_basis.T, precision=highest, preferred_element_type=f32)
    new_weight = weight - learn_rate * jnp.sqrt(f32(order) / f32(rank)) * update
    return new_momentum, new_weight, new_basis


def solution(mesh):
    return jax.shard_map(
        functools.partial(step, mesh),
        mesh=mesh,
        in_specs=(P("rep", "row", "col"), P("rep", "row", "col"), P("row", "col"), P("col", None)),
        out_specs=(P("rep", "row", "col"), P("row", "col"), P("col", None)),
        check_vma=False,
    )
```

time: 1770 us -> 140 us (0.08)
  waiting for transfers between devices: 1340 us -> 0 us
  blocking collectives: 260 us -> 0 us
  Pallas kernels: 0 us -> 131 us
  other arithmetic: 110 us -> 1.45 us
  matrix products: 25 us -> 5.4 us
    psum x4 -> x0, waiting for transfers between devices: 782 us -> none  [the longest x2 432 us: on_device(): gram_full = lax.psum(gram_part, 'row')]
    reduce_scatter x2 -> x0, waiting for transfers between devices: 516 us -> none  [on_device(): lax.psum_scatter(factor_part, ('row', 'rep'), scatter_dimension=0, tiled=...]
    psum x2 -> x0, blocking collectives: 260 us -> none  [on_device(): lax.psum(jnp.sum(wide_piece * wide_piece, axis=0), ('row', 'col', 'rep'))]
    pallas_call x0 -> x1, Pallas kernels: none -> 131 us  [step(): pl.pallas_call(functools.partial(step_kernel, (reps, cols, depth, m, n, s...]
    another operation x18 -> x0, other arithmetic: 108 us -> none  [the longest x13 68.6 us: on_device(): low_factor = jnp.linalg.cholesky(gram_full)]
    all_gather x2 -> x0, waiting for transfers between devices: 40.6 us -> none  [on_device(): factor = lax.all_gather(wide_piece, ('row', 'rep'), axis=0, tiled=True)]
  transfers between devices with their start and end apart: 8 -> 0, of which waited for: 8 -> 0; matrix products, arithmetic and copies ran while one was open for 0% -> 0% of each run, Pallas kernels for 0% -> 0%
where the time goes in v2:
time: 140 us
  Pallas kernels  131 us (94%)
  matrix products  5.4 us (4%)
  other arithmetic  1.45 us (1%)
    pallas_call x1, Pallas kernels, step(): pl.pallas_call(functools.partial(step_kernel, (reps, cols, depth, m, n, s...  131 us
    dot_general x1, matrix products, step(): jnp.dot(ortho, factor.T, precision=highest, preferred_element_type=f32)  3.35 us

profile of v2, /device:TPU:1, one launch (start us, length us, event | category | flops | bytes accessed | tf_op | source)
XLA Modules:
  0.0 139.7 jit_solution(10152145430867515335)
XLA Ops:
  0.6 0.0 copy-start.3
  0.6 131.1 %dion_step.1 = (f32[256,256]{1,0:T(8,128)}, f32[1024,256]{1,0:T(8,128)}, f32[8,256]{1,0:T(8,128)}) custom-call(f32[1,256,1024]{2,1,0:T(8,128)} %momentum_in.1, bf16[1,256,1024]{2,1,0:T(8,128)(2,1)} %gradient_in.1, f32[1024,256]{1,0:T(8,128)} %basis_in.1), custom_call_target="tpu_custom_call" | custom-call | tf_op jit(solution)/shard_map/dion_step/pallas_call | solution.py:432
  131.7 0.7 slice.3
  132.4 0.0 copy-start.1
  132.4 0.0 copy-start.2
  132.4 1.4 %broadcast_divide_fusion = f32[1024,256]{1,0:T(8,128)S(1)} fusion(f32[1024,256]{1,0:T(8,128)} %get-tuple-element.7, f32[256]{0:T(256)S(1)} %bitcast.9), kind=kLoop, calls=%fused_computation.5 | loop fusion | flops 262144 | bytes 2098176 | tf_op jit(solution)/shard_map/div | solution.py:455
  133.9 0.0 copy-done.3
  133.9 0.1 copy-done.1
  133.9 0.3 copy-done.2
  134.3 0.0 copy-start
  134.3 0.0 copy-start.4
  134.3 0.0 copy-start.5
  134.3 3.4 %fusion.2 = f32[1,256,1024]{2,1,0:T(8,128)} fusion(f32[256,256]{1,0:T(8,128)} %get-tuple-element.6, f32[1024,256]{1,0:T(8,128)S(1)} %copy-done.2, f32[1,256,1024]{2,1,0:T(8,128)S(1)} %copy-done.1, bf16[1,256,1024]{2,1,0:T(8,128)(2,1)S(1)} %copy-done.3), kind=kOutput, calls=%fused_computation.4 | convolution fusion | flops 806354944 | bytes 3932160 | tf_op jit(solution)/shard_map/dot_general | solution.py:456
  137.6 0.0 copy-done
  137.6 0.0 copy-done.4
  137.6 0.0 copy-done.5
  137.6 2.0 %fusion = f32[256,1024]{1,0:T(8,128)} fusion(f32[256,1024]{1,0:T(8,128)S(1)} %copy-done.4, f32[256,256]{1,0:T(8,128)S(1)} %copy-done.5, f32[1024,256]{1,0:T(8,128)S(1)} %broadcast_divide_fusion), kind=kOutput, calls=%fused_computation.1 | convolution fusion | flops 805830656 | bytes 3407872 | tf_op jit(solution)/shard_map/dot_general | solution.py:458
Async XLA Ops:
  0.6 133.2 %copy-start.3 = (bf16[1,256,1024]{2,1,0:T(8,128)(2,1)S(1)}, bf16[1,256,1024]{2,1,0:T(8,128)(2,1)}, u32[]{:S(2)}) copy-start(bf16[1,256,1024]{2,1,0:T(8,128)(2,1)} %gradient_in.1) | copy-start | bytes 1572868
  132.4 1.5 %copy-start.1 = (f32[1,256,1024]{2,1,0:T(8,128)S(1)}, f32[1,256,1024]{2,1,0:T(8,128)}, u32[]{:S(2)}) copy-start(f32[1,256,1024]{2,1,0:T(8,128)} %momentum_in.1) | copy-start | bytes 3145732
  132.4 1.9 %copy-start.2 = (f32[1024,256]{1,0:T(8,128)S(1)}, f32[1024,256]{1,0:T(8,128)}, u32[]{:S(2)}) copy-start(f32[1024,256]{1,0:T(8,128)} %get-tuple-element.7) | copy-start | bytes 3145732
  134.3 3.4 %copy-start = (f32[1024,256]{1,0:T(8,128)}, f32[1024,256]{1,0:T(8,128)S(1)}, u32[]{:S(2)}) copy-start(f32[1024,256]{1,0:T(8,128)S(1)} %broadcast_divide_fusion) | copy-start | bytes 3145732
  134.3 3.4 %copy-start.4 = (f32[256,1024]{1,0:T(8,128)S(1)}, f32[256,1024]{1,0:T(8,128)}, u32[]{:S(2)}) copy-start(f32[256,1024]{1,0:T(8,128)} %param.6) | copy-start | bytes 3145732
  134.3 3.4 %copy-start.5 = (f32[256,256]{1,0:T(8,128)S(1)}, f32[256,256]{1,0:T(8,128)}, u32[]{:S(2)}) copy-start(f32[256,256]{1,0:T(8,128)} %get-tuple-element.6) | copy-start | bytes 786436

commit v3 on v2

--- a/solution.py
+++ b/solution.py
@@ -184,34 +184,39 @@
     used = [0]
     pending = []
 
-    def send(group, source, target, mine):
-        first = used[0]
-        members = groups[group]
-        used[0] += len(members)
-        for i, (peer, origin, device) in enumerate(members):
-            copy = pltpu.make_async_remote_copy(
+    def send(group, source, target, mine, every):
+        index = used[0]
+        used[0] += 1
+        for peer, _, device in groups[group]:
+            pltpu.make_async_remote_copy(
                 src_ref=source(peer),
                 dst_ref=target(mine),
-                send_sem=sent.at[first + i],
-                recv_sem=wire.at[first + i],
+                send_sem=sent.at[index],
+                recv_sem=wire.at[index],
                 device_id=device,
                 device_id_type=MESH,
-            )
-            copy.start()
-            pending.append(copy)
+            ).start()
+        whole = pltpu.make_async_remote_copy(
+            src_ref=every,
+            dst_ref=every,
+            send_sem=sent.at[index],
+            recv_sem=wire.at[index],
+            device_id=groups[group][0][2],
+            device_id_type=MESH,
+        )
+        pending.append(whole)
 
         def wait():
-            for i, (peer, origin, device) in enumerate(members):
-                pltpu.make_async_remote_copy(
-                    src_ref=source(origin),
-                    dst_ref=target(origin),
-                    send_sem=sent.at[first + i],
-                    recv_sem=wire.at[first + i],
-                    device_id=device,
-                    device_id_type=MESH,
-                ).wait_recv()
+            whole.wait_recv()
 
         return wait
+
+    def others(ref):
+        return ref.at[pl.ds(0, ref.shape[0] - 1)]
+
+    def sends_done():
+        while pending:
+            pending.pop(0).wait_send()
 
     loads = [
         pltpu.make_async_copy(momentum_in.at[0], mem["momentum"], local.at[0]),
@@ -229,12 +234,9 @@
     for load in loads:
         load.wait()
 
-    product = None
     for k in range(reps):
         lanes = slice(k * sub, (k + 1) * sub)
         mem["piece"][k] = mem["momentum"][:, lanes] + gradient[:, lanes].astype(jnp.float32)
-        term = rows_by_rows(mem["piece"][k], mem["basis"][lanes, :])
-        product = term if product is None else product + term
 
     def added(ref):
         total = ref[0]
@@ -245,14 +247,14 @@
     def scatter_left(it, partial):
         out, got = mem["left_part"].at[it], mem["left_got"].at[it]
         out[...] = partial.reshape(plane, part, rank)
-        wait = send("xy", lambda p: out.at[p], lambda s: got.at[s], here)
+        wait = send("xy", lambda p: out.at[p], lambda s: got.at[s], here, others(got))
         got[here] = out[here]
         return wait
 
     def gather_left(it):
         full = mem["left"].at[it]
         full[here] = added(mem["left_got"].at[it])
-        return send("xy", lambda p: full.at[here], lambda s: full.at[s], here)
+        return send("xy", lambda p: full.at[here], lambda s: full.at[s], here, others(full))
 
     def left_of(it):
         return mem["left"][it].reshape(m, rank)
@@ -267,38 +269,50 @@
 
         mean_t = mem["mean_t"][...]
         split[0] = rows_by_rows(mean_t, now[:, lanes_of(sibling)])
-        wait_c = send("c", lambda p: split.at[0], lambda s: other.at[0], 0)
+        wait_c = send("c", lambda p: split.at[0], lambda s: other, 0, other)
         split[1] = rows_by_rows(mean_t, now[:, lanes_of(core)])
+        wait_c()
+        out, got = mem["right_z"].at[it], mem["right_got"].at[it]
+        out[...] = (split[1] + other[...]).reshape(depth, part_z, half)
+        wait_c = send("z", lambda p: out.at[p], lambda s: got.at[s], z, others(got))
+        got[z] = out[z]
         mem["gram_part"][it] = transposed_by(now[...], now[...])
         mine = pl.ds(pl.multiple_of(here * part_g, TILE), part_g)
         g_out, g_other = mem["gram_split"].at[it], mem["gram_core"].at[it]
         g_out[...] = mem["gram_part"][it, mine, lanes_of(sibling)]
-        wait_g = send("c", lambda p: g_out, lambda s: g_other, 0)
-        wait_c()
-        out, got = mem["right_z"].at[it], mem["right_got"].at[it]
-        out[...] = (split[1] + other[0]).reshape(depth, part_z, half)
-        wait_c = send("z", lambda p: out.at[p], lambda s: got.at[s], z)
-        got[z] = out[z]
+        wait_g = send("c", lambda p: g_out, lambda s: g_other, 0, g_other)
         wait_g()
         g_all = mem["gram_z"].at[it]
         g_all[z] = mem["gram_part"][it, mine, lanes_of(core)] + g_other[...]
-        wait_g = send("z", lambda p: g_all.at[z], lambda s: g_all.at[s], z)
+        wait_g = send("z", lambda p: g_all.at[z], lambda s: g_all.at[s], z, others(g_all))
         yield
         wait_c()
         full = mem["right"].at[it]
         full[core, z] = added(got)
-        wait_c = send("z", lambda p: full.at[core, z], lambda s: full.at[core, s], z)
+        wait_c = send(
+            "z", lambda p: full.at[core, z], lambda s: full.at[core, s], z, others(full.at[core])
+        )
         wait_g()
         gram = mem["gram"].at[it]
         gram[core, here] = added(g_all)
-        wait_g = send("xy", lambda p: gram.at[core, here], lambda s: gram.at[core, s], here)
+        wait_g = send(
+            "xy",
+            lambda p: gram.at[core, here],
+            lambda s: gram.at[core, s],
+            here,
+            others(gram.at[core]),
+        )
         yield
         wait_c()
-        wait_c = send("c", lambda p: full.at[core], lambda s: full.at[s], core)
+        if it == 0:
+            wait_c = send("c", lambda p: full.at[core], lambda s: full.at[s], core, full.at[0])
+        else:
+            rights = mem["rights"].at[core]
+            rights[x] = full[core]
+            wait_c = send("x", lambda p: full.at[core], lambda s: rights.at[s], x, others(rights))
         wait_g()
-        wait_g = send("c", lambda p: gram.at[core], lambda s: gram.at[s], core)
-        wait_c()
-        yield
+        wait_g = send("c", lambda p: gram.at[core], lambda s: gram.at[s], core, gram.at[0])
+        yield wait_c
         wait_g()
 
     def joined(ref, rows):
@@ -311,7 +325,7 @@
     def share(group, name, mine, value):
         ref = mem[name]
         ref[mine] = value
-        return send(group, lambda p: ref.at[mine], lambda s: ref.at[s], mine)
+        return send(group, lambda p: ref.at[mine], lambda s: ref.at[s], mine, others(ref))
 
     def rms_of(total):
         return jnp.sqrt(total / jnp.float32(order) + 1e-06)
@@ -319,9 +333,15 @@
     chol = Cholesky(mem["chol"])
     middle = chol.groups // 2
 
+    product = None
+    for k in range(reps):
+        term = rows_by_rows(mem["piece"][k], mem["basis"][k * sub : (k + 1) * sub, :])
+        product = term if product is None else product + term
     pl.semaphore_wait(barrier, partners)
     wait_left = scatter_left(0, product * (1.0 / reps))
-    exchange = send("x", lambda p: mem["piece"].at[p], lambda s: mem["pieces"].at[s], x)
+    exchange = send(
+        "x", lambda p: mem["piece"].at[p], lambda s: mem["pieces"].at[s], x, others(mem["pieces"])
+    )
     mem["pieces"][x] = mem["piece"][x]
     wait_left()
     wait_left = gather_left(0)
@@ -334,7 +354,7 @@
     stages = reduce_right(0)
     next(stages)
     next(stages)
-    next(stages)
+    next(stages)()
     right = joined(mem["right"].at[0], sub)
     wait_left = scatter_left(1, rows_by_rows(mem["mean"][...], right))
     for _ in stages:
@@ -356,10 +376,8 @@
     next(stages)
     wait_squares()
     wait_squares = share("y", "square_y", y, added(mem["square_x"]))
-    next(stages)
-    gathered = mem["rights"]
-    gathered[x] = mem["right"][1]
-    wait_right = send("x", lambda p: mem["right"].at[1], lambda s: gathered.at[s], x)
+    sends_done()
+    wait_right = next(stages)
     wait_squares()
     scale = (1.0 / rms_of(added(mem["square_y"])))[:1, :]
     mem["scale"][...] = jnp.broadcast_to(scale, (TILE, rank))
@@ -368,23 +386,53 @@
         pass
     chol.load(joined(mem["gram"].at[1], rank) * scale * across)
     chol.run(0, middle)
+    wait_right()
+    rights = mem["rights"]
+    wait_right = send(
+        "c", lambda p: rights.at[core], lambda s: rights.at[s], core, rights.at[0]
+    )
     chol.run(middle, chol.groups)
     inverse = chol.inverse()
     scale = mem["scale"][:1, :]
     wait_right()
     squares = None
     for k in range(reps):
-        factor = by_transposed(joined(gathered.at[k], sub) * scale, inverse)
+        gathered = [rights[h, k].reshape(sub, half) for h in range(CORES)]
+        factor = by_transposed(jnp.concatenate(gathered, axis=1) * scale, inverse)
         factor_out[k * sub : (k + 1) * sub, :] = factor
         term = squares_of(factor)
         squares = term if squares is None else squares + term
     wait_squares = share("y", "square_last", y, squares)
     ortho_out[...] = by_transposed(mem["now"][...] * scale, inverse)
-    for copy in pending:
-        copy.wait_send()
+    sends_done()
     wait_squares()
     rms_out[...] = rms_of(added(mem["square_last"]))
     assert used[0] == sent.shape[0]
+
+
+def in_two(x):
+    high = x.astype(jnp.bfloat16)
+    return high, (x - high.astype(jnp.float32)).astype(jnp.bfloat16)
+
+
+def three_products(a, b):
+    (ah, al), (bh, bl) = a, b
+
+    def one(p, q):
+        return lax.dot_general(
+            p, q, (((1,), (1,)), ((), ())), preferred_element_type=jnp.float32
+        )
+
+    return (one(al, bh) + one(ah, bl)) + one(ah, bh)
+
+
+def finish_kernel(rate, ortho, rms, factor, momentum, gradient, weight, new_momentum, new_weight, new_basis):
+    basis = factor[...] / rms[:1, :]
+    new_basis[...] = basis
+    left = in_two(ortho[...])
+    buffer = momentum[0] + gradient[0].astype(jnp.float32)
+    new_momentum[0] = buffer - (1.0 - beta_mom) * three_products(left, in_two(factor[...]))
+    new_weight[...] = weight[...] - rate * three_products(left, in_two(basis))
 
 
 def step(mesh, momentum, gradient, weight, right_basis):
@@ -409,7 +457,7 @@
         "now": (m, rank),
         "gram_part": (2, rank, rank),
         "right_split": (2, CORES, sub, half),
-        "right_core": (2, 1, sub, half),
+        "right_core": (2, sub, half),
         "gram_split": (2, part_g, half),
         "gram_core": (2, part_g, half),
         "right_z": (2, depth, part_z, half),
@@ -422,11 +470,9 @@
         "square_last": (cols, TILE, rank),
         "scale": (TILE, rank),
         "chol": (rank, 2 * rank),
-        "rights": (reps, CORES, depth, part_z, half),
+        "rights": (CORES, reps, depth, part_z, half),
     }
-    links = {"x": reps - 1, "y": cols - 1, "z": depth - 1, "c": CORES - 1, "xy": plane - 1}
-    copies = 2 * (3 * links["xy"] + 3 * links["z"] + 4 * links["c"] + links["x"] + links["y"])
-    copies += links["x"]
+    copies = 25
     hbm = pl.BlockSpec(memory_space=pl.ANY)
     vmem = pl.BlockSpec(memory_space=pltpu.VMEM)
     ortho, factor, rms = pl.pallas_call(
@@ -450,14 +496,25 @@
         ),
         name="dion_step",
     )(momentum, gradient, right_basis)
-    highest = lax.Precision.HIGHEST
-    buffer = momentum[0] + gradient[0].astype(f32)
-    new_basis = factor / rms[:1, :]
-    feedback = jnp.dot(ortho, factor.T, precision=highest, preferred_element_type=f32)
-    new_momentum = (buffer - (1.0 - beta_mom) * feedback)[None]
-    update = jnp.dot(ortho, new_basis.T, precision=highest, preferred_element_type=f32)
-    new_weight = weight - learn_rate * jnp.sqrt(f32(order) / f32(rank)) * update
-    return new_momentum, new_weight, new_basis
+    tile = min(256, n)
+    whole = pl.BlockSpec((m, rank), lambda i: (0, 0))
+    plain = pl.BlockSpec((m, tile), lambda i: (0, i))
+    stack = pl.BlockSpec((1, m, tile), lambda i: (0, 0, i))
+    lines = pl.BlockSpec((tile, rank), lambda i: (i, 0))
+    rate = learn_rate * (order / rank) ** 0.5
+    return pl.pallas_call(
+        functools.partial(finish_kernel, rate),
+        grid=(n // tile,),
+        out_shape=[
+            jax.ShapeDtypeStruct((1, m, n), f32),
+            jax.ShapeDtypeStruct((m, n), f32),
+            jax.ShapeDtypeStruct((n, rank), f32),
+        ],
+        in_specs=[whole, pl.BlockSpec((TILE, rank), lambda i: (0, 0)), lines, stack, stack, plain],
+        out_specs=[stack, plain, lines],
+        compiler_params=pltpu.CompilerParams(vmem_limit_bytes=58 << 20),
+        name="dion_finish",
+    )(ortho, rms, factor, momentum, gradient, weight)
 
 
 def solution(mesh):

time: 140 us -> 129 us (0.921)
  matrix products: 5.4 us -> 0 us
  Pallas kernels: 131 us -> 128 us
  other arithmetic: 1.45 us -> 0 us
    pallas_call x1, Pallas kernels: 131 us -> 123 us  [step(): pl.pallas_call(functools.partial(step_kernel, (reps, cols, depth, m, n, s...]
    dot_general x2 -> x0, matrix products: 5.4 us -> none  [the longest x1 3.35 us: step(): jnp.dot(ortho, factor.T, precision=highest, preferred_element_type=f32)]
    pallas_call x0 -> x1, Pallas kernels: none -> 5.29 us  [step(): pl.pallas_call(functools.partial(finish_kernel, rate), grid=(n // tile,),...]
    div x1 -> x0, other arithmetic: 1.45 us -> none  [step(): new_basis = factor / rms[:1, :]]
where the time goes in v3:
time: 129 us
  Pallas kernels  128 us (99%)
    pallas_call x1, Pallas kernels, step(): pl.pallas_call(functools.partial(step_kernel, (reps, cols, depth, m, n, s...  123 us
    pallas_call x1, Pallas kernels, step(): pl.pallas_call(functools.partial(finish_kernel, rate), grid=(n // tile,),...  5.29 us

profile of v3, /device:TPU:1, one launch (start us, length us, event | category | flops | bytes accessed | tf_op | source)
XLA Modules:
  0.0 128.9 jit_solution(9787369417442867035)
XLA Ops:
  0.6 122.9 %dion_step.1 = (f32[256,256]{1,0:T(8,128)}, f32[1024,256]{1,0:T(8,128)}, f32[8,256]{1,0:T(8,128)}) custom-call(f32[1,256,1024]{2,1,0:T(8,128)} %momentum.1, bf16[1,256,1024]{2,1,0:T(8,128)(2,1)} %gradient.1, f32[1024,256]{1,0:T(8,128)} %basis_in.1), custom_call_target="tpu_custom_call" | custom-call | tf_op jit(solution)/shard_map/dion_step/pallas_call | solution.py:478
  123.6 5.3 %dion_finish.1 = (f32[1,256,1024]{2,1,0:T(8,128)}, f32[256,1024]{1,0:T(8,128)}, f32[1024,256]{1,0:T(8,128)}) custom-call(f32[256,256]{1,0:T(8,128)} %get-tuple-element.6.ortho, f32[8,256]{1,0:T(8,128)} %get-tuple-element.7.rms, f32[1024,256]{1,0:T(8,128)} %get-tuple-element.8.factor, f32[1,256,1024]{2,1,0:T(8,128)} %momentum.1, ...), custom_call_target="tpu_custom_call" | custom-call | tf_op jit(solution)/shard_map/dion_finish/pallas_call | solution.py:505

commit v4 on v3

--- a/solution.py
+++ b/solution.py
@@ -304,16 +304,70 @@
         )
         yield
         wait_c()
-        if it == 0:
-            wait_c = send("c", lambda p: full.at[core], lambda s: full.at[s], core, full.at[0])
-        else:
-            rights = mem["rights"].at[core]
-            rights[x] = full[core]
-            wait_c = send("x", lambda p: full.at[core], lambda s: rights.at[s], x, others(rights))
+        wait_c = send("c", lambda p: full.at[core], lambda s: full.at[s], core, full.at[0])
         wait_g()
         wait_g = send("c", lambda p: gram.at[core], lambda s: gram.at[s], core, gram.at[0])
         yield wait_c
         wait_g()
+
+    def reduce_right_gram_first():
+        it, now = 1, mem["now"]
+        split, other = mem["right_split"].at[it], mem["right_core"].at[it]
+        sibling = CORES - 1 - core
+
+        def lanes_of(h):
+            return pl.ds(pl.multiple_of(h * half, half), half)
+
+        mem["gram_part"][it] = transposed_by(now[...], now[...])
+        mine = pl.ds(pl.multiple_of(here * part_g, TILE), part_g)
+        g_out, g_other = mem["gram_split"].at[it], mem["gram_core"].at[it]
+        g_out[...] = mem["gram_part"][it, mine, lanes_of(sibling)]
+        wait_g = send("c", lambda p: g_out, lambda s: g_other, 0, g_other)
+        mean_t = mem["mean_t"][...]
+        split[0] = rows_by_rows(mean_t, now[:, lanes_of(sibling)])
+        wait_c = send("c", lambda p: split.at[0], lambda s: other, 0, other)
+        wait_g()
+        g_all = mem["gram_z"].at[it]
+        g_all[z] = mem["gram_part"][it, mine, lanes_of(core)] + g_other[...]
+        wait_g = send("z", lambda p: g_all.at[z], lambda s: g_all.at[s], z, others(g_all))
+        split[1] = rows_by_rows(mean_t, now[:, lanes_of(core)])
+        wait_c()
+        out, got = mem["right_z"].at[it], mem["right_got"].at[it]
+        out[...] = (split[1] + other[...]).reshape(depth, part_z, half)
+        wait_c = send("z", lambda p: out.at[p], lambda s: got.at[s], z, others(got))
+        got[z] = out[z]
+        yield
+        wait_g()
+        gram = mem["gram"].at[it]
+        gram[core, here] = added(g_all)
+        wait_g = send(
+            "xy",
+            lambda p: gram.at[core, here],
+            lambda s: gram.at[core, s],
+            here,
+            others(gram.at[core]),
+        )
+        wait_c()
+        full = mem["right"].at[it]
+        full[core, z] = added(got)
+        wait_c = send(
+            "z", lambda p: full.at[core, z], lambda s: full.at[core, s], z, others(full.at[core])
+        )
+        yield
+        wait_g()
+        wait_g = send("c", lambda p: gram.at[core], lambda s: gram.at[s], core, gram.at[0])
+        wait_g()
+        yield
+        wait_c()
+        rights = mem["rights"]
+        by_x = rights.at[core]
+        by_x[x] = full[core]
+        wait_c = send("x", lambda p: full.at[core], lambda s: by_x.at[s], x, others(by_x))
+        yield
+        wait_c()
+        wait_c = send("c", lambda p: rights.at[core], lambda s: rights.at[s], core, rights.at[0])
+        yield
+        wait_c()
 
     def joined(ref, rows):
         return jnp.concatenate([ref[h].reshape(rows, half) for h in range(CORES)], axis=1)
@@ -369,7 +423,7 @@
     left = by_transposed(left_of(1), inverse)
     mem["now"][...] = left
 
-    stages = reduce_right(1)
+    stages = reduce_right_gram_first()
     next(stages)
     squares = squares_of(by_transposed(joined(mem["right"].at[0], sub), inverse))
     wait_squares = share("x", "square_x", x, squares)
@@ -377,24 +431,23 @@
     wait_squares()
     wait_squares = share("y", "square_y", y, added(mem["square_x"]))
     sends_done()
-    wait_right = next(stages)
     wait_squares()
     scale = (1.0 / rms_of(added(mem["square_y"])))[:1, :]
     mem["scale"][...] = jnp.broadcast_to(scale, (TILE, rank))
     across = jnp.transpose(jnp.broadcast_to(scale, (LANES, rank)))[:, :1]
+    next(stages)
+    chol.load(joined(mem["gram"].at[1], rank) * scale * across)
+    rights = mem["rights"]
+    chol.run(0, 1)
+    next(stages)
+    chol.run(1, middle)
+    chol.run(middle, chol.groups - 2)
+    next(stages)
+    chol.run(chol.groups - 2, chol.groups)
+    inverse = chol.inverse()
+    scale = mem["scale"][:1, :]
     for _ in stages:
         pass
-    chol.load(joined(mem["gram"].at[1], rank) * scale * across)
-    chol.run(0, middle)
-    wait_right()
-    rights = mem["rights"]
-    wait_right = send(
-        "c", lambda p: rights.at[core], lambda s: rights.at[s], core, rights.at[0]
-    )
-    chol.run(middle, chol.groups)
-    inverse = chol.inverse()
-    scale = mem["scale"][:1, :]
-    wait_right()
     squares = None
     for k in range(reps):
         gathered = [rights[h, k].reshape(sub, half) for h in range(CORES)]

time: 129 us -> 129 us (level)
  no operation moved by 1% of the time
where the time goes in v4:
time: 129 us; the launch traced here: 128 us
  Pallas kernels  128 us (99%)
    pallas_call x1, Pallas kernels, step(): pl.pallas_call(functools.partial(step_kernel, (reps, cols, depth, m, n, s...  122 us
    pallas_call x1, Pallas kernels, step(): pl.pallas_call(functools.partial(finish_kernel, rate), grid=(n // tile,),...  5.29 us

profile of v4, /device:TPU:1, one launch (start us, length us, event | category | flops | bytes accessed | tf_op | source)
XLA Modules:
  0.0 128.3 jit_solution(4101172736415743072)
XLA Ops:
  0.6 122.3 %dion_step.1 = (f32[256,256]{1,0:T(8,128)}, f32[1024,256]{1,0:T(8,128)}, f32[8,256]{1,0:T(8,128)}) custom-call(f32[1,256,1024]{2,1,0:T(8,128)} %momentum.1, bf16[1,256,1024]{2,1,0:T(8,128)(2,1)} %gradient.1, f32[1024,256]{1,0:T(8,128)} %basis_in.1), custom_call_target="tpu_custom_call" | custom-call | tf_op jit(solution)/shard_map/dion_step/pallas_call | solution.py:531
  123.0 5.3 %dion_finish.1 = (f32[1,256,1024]{2,1,0:T(8,128)}, f32[256,1024]{1,0:T(8,128)}, f32[1024,256]{1,0:T(8,128)}) custom-call(f32[256,256]{1,0:T(8,128)} %get-tuple-element.6.ortho, f32[8,256]{1,0:T(8,128)} %get-tuple-element.7.rms, f32[1024,256]{1,0:T(8,128)} %get-tuple-element.8.factor, f32[1,256,1024]{2,1,0:T(8,128)} %momentum.1, ...), custom_call_target="tpu_custom_call" | custom-call | tf_op jit(solution)/shard_map/dion_finish/pallas_call | solution.py:558
